TPU v7x, 32 devices: a whole 2x2x4 slice. The times are simulated.
32 devices in a mesh: group: 4 (over z), replica: 8 (over y, x, core).
Axes of the slice: x: 2, y: 2, z: 4, core: 2. Of those that a mesh axis runs over, the one named last changes fastest.
Arguments:
- layer_input: bfloat16 [8, 1024, 2560], P('replica', 'group')
- positions: int32 [8, 1024], P('replica', 'group'), may hold values from 0 to 543, as said below
- piece_starts: int32 [8, 2], P('replica'), may hold values from 0 to 768, as said below
- gain_attn: bfloat16 [2560], P('group'), may hold values from 0.5 to 1.5
- w_query: bfloat16 [2560, 2560], P('group'), may hold values from -0.125 to 0.125
- w_key: bfloat16 [2560, 640], P('group'), may hold values from -0.125 to 0.125
- w_value: bfloat16 [2560, 640], P('group'), may hold values from -0.125 to 0.125
- w_out: bfloat16 [2560, 2560], P('group'), may hold values from -2 to 2
- gain_mlp: bfloat16 [2560], P('group'), may hold values from 0.5 to 1.5
- w_gate: bfloat16 [2560, 7168], P('group'), may hold values from -0.125 to 0.125
- w_up: bfloat16 [2560, 7168], P('group'), may hold values from -0.125 to 0.125
- w_down: bfloat16 [2560, 7168], P('group'), may hold values from -0.0625 to 0.0625
- out_grad: bfloat16 [8, 1024, 2560], P('replica', 'group'), may hold values from -6 to 6
Outputs:
- layer_out: bfloat16 [8, 1024, 2560], P('replica', 'group')
- input_grad: float32 [8, 1024, 2560], P('replica', 'group')
- grad_norm_attn: float32 [2560], P(('group', 'replica'))
- grad_query: float32 [2560, 2560], P(('group', 'replica'))
- grad_key: float32 [2560, 640], P(('group', 'replica'))
- grad_value: float32 [2560, 640], P(('group', 'replica'))
- grad_out: float32 [2560, 2560], P(('group', 'replica'))
- grad_norm_mlp: float32 [2560], P(('group', 'replica'))
- grad_gate: float32 [2560, 7168], P(('group', 'replica'))
- grad_up: float32 [2560, 7168], P(('group', 'replica'))
- grad_down: float32 [2560, 7168], P(('group', 'replica'))
- stream_rms: float32 [8, 3], P('replica')
Inputs may be any that keep to these rules, and one draw needn't show every extreme that they name: `piece_starts`: each sequence holds two picture pieces of 256 tokens that start at multiples of 128, the second starting 256 or more tokens after the first, both ending inside the sequence. `positions`: outside picture pieces a token's position is one more than the previous token's; the j-th token of a piece whose first token has position p gets p + j // 16, and the token after the piece gets p + 16; a sequence's first token has position 0.
All inputs are finite; a program needn't handle non-finite values.
Results may differ from a plain program's by a relative error of at most 0.018.
Values may be sent and summed in bfloat16 or wider, within the bound.
No kernel may reach another device: no remote copies, remote signals or barrier semaphores. Data moves between devices by JAX's collectives and lax.ppermute only.
A program may use at most 384 MiB of HBM per device.

v0:
```python
import jax
import jax.numpy as jnp
from jax import lax
from jax.sharding import PartitionSpec as P

HEADS = 32
KV_HEADS = 8
HEAD_DIM = 80
PIECE = 256
epsilon = 1e-05
rope_base = 1000000.0


def rope_tables(places):
    halves = HEAD_DIM // 2
    frequency = rope_base ** (-(jnp.arange(halves, dtype=jnp.float32) * 2.0 / HEAD_DIM))
    angles = places.astype(jnp.float32)[..., None] * frequency
    angles = jnp.concatenate([angles, angles], axis=-1)
    return (jnp.cos(angles), jnp.sin(angles))


def rotate(values, cosine, sine):
    halves = HEAD_DIM // 2
    turned = jnp.concatenate([-values[..., halves:], values[..., :halves]], axis=-1)
    return values * cosine[:, :, None, :] + turned * sine[:, :, None, :]


def unrotate(grads, cosine, sine):
    halves = HEAD_DIM // 2
    shifted = grads * sine[:, :, None, :]
    turned = jnp.concatenate([shifted[..., halves:], -shifted[..., :halves]], axis=-1)
    return grads * cosine[:, :, None, :] + turned


def times_t(left, right):
    return lax.dot_general(
        left, right, (((1,), (1,)), ((), ())), preferred_element_type=jnp.float32
    )


def inner_t(left, right):
    return lax.dot_general(
        left, right, (((0,), (0,)), ((), ())), preferred_element_type=jnp.float32
    )


def inverse_rms(values):
    return lax.rsqrt(jnp.mean(values * values, axis=-1, keepdims=True) + epsilon)


def norm_back(grad_normed, source, inverse, gain_full):
    weighted = grad_normed * gain_full
    average = jnp.mean(weighted * source, axis=-1, keepdims=True)
    return inverse * weighted - source * (inverse * inverse * inverse) * average


def piece_index(starts, places):
    labels = jnp.zeros(places.shape, jnp.int32)
    for which in range(2):
        inside = (places >= starts[which]) & (places < starts[which] + PIECE)
        labels = jnp.where(inside, which + 1, labels)
    return labels


def shards(
    layer_input,
    positions,
    piece_starts,
    gain_attn,
    w_query,
    w_key,
    w_value,
    w_out,
    gain_mlp,
    w_gate,
    w_up,
    w_down,
    out_grad,
):
    sequences, block_size, model_width = layer_input.shape
    token_rows = sequences * block_size
    kv_width = KV_HEADS * HEAD_DIM
    repeats = HEADS // KV_HEADS
    scaling = HEAD_DIM ** (-0.5)
    full_len = block_size * lax.axis_size("group")
    source = layer_input.astype(jnp.float32).reshape(token_rows, model_width)
    inverse_one = inverse_rms(source)
    unit_one = source * inverse_one
    gain_piece = lax.all_gather(gain_attn, "group", axis=0, tiled=True)
    query_piece = lax.all_gather(w_query, "group", axis=0, tiled=True)
    key_piece = lax.all_gather(w_key, "group", axis=0, tiled=True)
    value_piece = lax.all_gather(w_value, "group", axis=0, tiled=True)
    out_piece = lax.all_gather(w_out, "group", axis=0, tiled=True)
    scaled = unit_one * gain_piece.astype(jnp.float32)
    scaled = scaled.astype(jnp.bfloat16)
    query = jnp.dot(scaled, query_piece, preferred_element_type=jnp.float32)
    keyed = jnp.dot(scaled, key_piece, preferred_element_type=jnp.float32)
    valued = jnp.dot(scaled, value_piece, preferred_element_type=jnp.float32)
    normed = scaled
    gains = gain_piece
    out_full = out_piece
    query_lin, key_lin, value_lin, normed_one, gain_one_low, out_full = (
        query,
        keyed,
        valued,
        normed,
        gains,
        out_full,
    )
    gain_one = gain_one_low.astype(jnp.float32)
    cosine, sine = rope_tables(positions)
    query_rot = rotate(
        query_lin.reshape(sequences, block_size, HEADS, HEAD_DIM), cosine, sine
    ).astype(jnp.bfloat16)
    key_rot = rotate(
        key_lin.reshape(sequences, block_size, KV_HEADS, HEAD_DIM), cosine, sine
    ).astype(jnp.bfloat16)
    key_rot = key_rot.reshape(sequences, block_size, kv_width)
    value_low = value_lin.astype(jnp.bfloat16).reshape(sequences, block_size, kv_width)
    key_all, value_all = (
        lax.all_gather(key_rot, "group", axis=1, tiled=True),
        lax.all_gather(value_low, "group", axis=1, tiled=True),
    )
    query_places = lax.axis_index("group") * block_size + jnp.arange(block_size, dtype=jnp.int32)
    key_places = jnp.arange(full_len, dtype=jnp.int32)

    def allowed_for(starts):
        query_labels = piece_index(starts, query_places)
        key_labels = piece_index(starts, key_places)
        causal = key_places[None, :] <= query_places[:, None]
        same_piece = (query_labels[:, None] == key_labels[None, :]) & (query_labels[:, None] > 0)
        return causal | same_piece

    def scores_of(query_seq, key_seq, starts):
        grouped = query_seq.reshape(block_size, KV_HEADS, repeats, HEAD_DIM)
        keys_grouped = key_seq.reshape(full_len, KV_HEADS, HEAD_DIM)
        raw = (
            jnp.einsum("qkrd,skd->krqs", grouped, keys_grouped, preferred_element_type=jnp.float32)
            * scaling
        )
        return jnp.where(allowed_for(starts)[None, None], raw, -1e30)

    def attend_one(packed):
        query_seq, key_seq, value_seq, starts = packed
        masked = scores_of(query_seq, key_seq, starts)
        highest_score = jnp.max(masked, axis=-1, keepdims=True)
        raised = jnp.exp(masked - highest_score)
        summed = jnp.sum(raised, axis=-1, keepdims=True)
        chances_low = (raised / summed).astype(jnp.bfloat16)
        values_grouped = value_seq.reshape(full_len, KV_HEADS, HEAD_DIM)
        mixed = jnp.einsum(
            "krqs,skd->qkrd", chances_low, values_grouped, preferred_element_type=jnp.float32
        )
        return (mixed.reshape(block_size, model_width), highest_score + jnp.log(summed))

    mixed_all, log_totals = lax.map(attend_one, (query_rot, key_all, value_all, piece_starts))
    mixed_low = mixed_all.reshape(token_rows, model_width).astype(jnp.bfloat16)
    middle = source + times_t(mixed_low, out_full)
    inverse_two = inverse_rms(middle)
    unit_two = middle * inverse_two
    gain_piece = lax.all_gather(gain_mlp, "group", axis=0, tiled=True)
    gate_piece = lax.all_gather(w_gate, "group", axis=0, tiled=True)
    up_piece = lax.all_gather(w_up, "group", axis=0, tiled=True)
    down_piece = lax.all_gather(w_down, "group", axis=0, tiled=True)
    scaled = unit_two * gain_piece.astype(jnp.float32)
    scaled = scaled.astype(jnp.bfloat16)
    gated = jnp.dot(scaled, gate_piece, preferred_element_type=jnp.float32)
    lifted = jnp.dot(scaled, up_piece, preferred_element_type=jnp.float32)
    normed = scaled
    gains = gain_piece
    down_full = down_piece
    gated, lifted, normed_two, gain_two_low, down_full = (gated, lifted, normed, gains, down_full)
    gain_two = gain_two_low.astype(jnp.float32)
    activated = jax.nn.silu(gated)
    hidden = (activated * lifted).astype(jnp.bfloat16)
    output_full = middle + times_t(hidden, down_full)
    grad_low = out_grad.reshape(token_rows, model_width)
    grad_top = grad_low.astype(jnp.float32)
    grad_hidden = jnp.dot(grad_low, down_full, preferred_element_type=jnp.float32)
    sigmoid_gate = jax.nn.sigmoid(gated)
    grad_gate_low = (
        grad_hidden * lifted * (sigmoid_gate + gated * sigmoid_gate * (1.0 - sigmoid_gate))
    ).astype(jnp.bfloat16)
    grad_lift_low = (grad_hidden * activated).astype(jnp.bfloat16)
    gate_piece = lax.all_gather(w_gate, "group", axis=0, tiled=True)
    up_piece = lax.all_gather(w_up, "group", axis=0, tiled=True)
    added = times_t(grad_gate_low, gate_piece) + times_t(grad_lift_low, up_piece)
    grad_normed_two = added
    grad_gain_two = jnp.sum(grad_normed_two * unit_two, axis=0)
    grad_middle = grad_top + norm_back(grad_normed_two, middle, inverse_two, gain_two)
    grad_middle_low = grad_middle.astype(jnp.bfloat16)
    grad_mixed_low = jnp.dot(grad_middle_low, out_full, preferred_element_type=jnp.float32).astype(
        jnp.bfloat16
    )

    def attend_back(packed):
        query_seq, key_seq, value_seq, starts, log_total, grad_seq = packed
        masked = scores_of(query_seq, key_seq, starts)
        chances = jnp.exp(masked - log_total)
        grad_grouped = grad_seq.reshape(block_size, KV_HEADS, repeats, HEAD_DIM)
        values_grouped = value_seq.reshape(full_len, KV_HEADS, HEAD_DIM)
        keys_grouped = key_seq.reshape(full_len, KV_HEADS, HEAD_DIM)
        query_grouped = query_seq.reshape(block_size, KV_HEADS, repeats, HEAD_DIM)
        grad_value_seq = jnp.einsum(
            "krqs,qkrd->skd",
            chances.astype(jnp.bfloat16),
            grad_grouped,
            preferred_element_type=jnp.float32,
        )
        grad_chance = jnp.einsum(
            "qkrd,skd->krqs", grad_grouped, values_grouped, preferred_element_type=jnp.float32
        )
        grad_score = chances * (
            grad_chance - jnp.sum(chances * grad_chance, axis=-1, keepdims=True)
        )
        grad_score = grad_score.astype(jnp.bfloat16)
        grad_query_seq = (
            jnp.einsum(
                "krqs,skd->qkrd", grad_score, keys_grouped, preferred_element_type=jnp.float32
            )
            * scaling
        )
        grad_key_seq = (
            jnp.einsum(
                "krqs,qkrd->skd", grad_score, query_grouped, preferred_element_type=jnp.float32
            )
            * scaling
        )
        return (
            grad_query_seq.reshape(block_size, HEADS, HEAD_DIM),
            grad_key_seq.reshape(full_len, kv_width),
            grad_value_seq.reshape(full_len, kv_width),
        )

    grad_query_rot, grad_key_full, grad_value_full = lax.map(
        attend_back,
        (
            query_rot,
            key_all,
            value_all,
            piece_starts,
            log_totals,
            grad_mixed_low.reshape(sequences, block_size, model_width),
        ),
    )
    grad_key_rot, grad_value_sum = (
        lax.psum_scatter(grad_key_full, "group", scatter_dimension=1, tiled=True),
        lax.psum_scatter(grad_value_full, "group", scatter_dimension=1, tiled=True),
    )
    grad_query_low = (
        unrotate(grad_query_rot, cosine, sine).astype(jnp.bfloat16).reshape(token_rows, model_width)
    )
    grad_key_low = (
        unrotate(grad_key_rot.reshape(sequences, block_size, KV_HEADS, HEAD_DIM), cosine, sine)
        .astype(jnp.bfloat16)
        .reshape(token_rows, kv_width)
    )
    grad_value_low = grad_value_sum.astype(jnp.bfloat16).reshape(token_rows, kv_width)
    query_piece = lax.all_gather(w_query, "group", axis=0, tiled=True)
    key_piece = lax.all_gather(w_key, "group", axis=0, tiled=True)
    value_piece = lax.all_gather(w_value, "group", axis=0, tiled=True)
    added = (
        times_t(grad_query_low, query_piece)
        + times_t(grad_key_low, key_piece)
        + times_t(grad_value_low, value_piece)
    )
    grad_gain_one = jnp.sum(added * unit_one, axis=0)
    input_grad = grad_middle + norm_back(added, source, inverse_one, gain_one)
    normed_own, middle_own, normed_mlp_own, top_own = (
        lax.all_to_all(normed_one, "group", split_axis=1, concat_axis=0, tiled=True),
        lax.all_to_all(grad_middle_low, "group", split_axis=1, concat_axis=0, tiled=True),
        lax.all_to_all(normed_two, "group", split_axis=1, concat_axis=0, tiled=True),
        lax.all_to_all(grad_low, "group", split_axis=1, concat_axis=0, tiled=True),
    )
    query_rows, key_rows, value_rows, mixed_rows = (
        lax.all_gather(grad_query_low, "group", axis=0, tiled=True),
        lax.all_gather(grad_key_low, "group", axis=0, tiled=True),
        lax.all_gather(grad_value_low, "group", axis=0, tiled=True),
        lax.all_gather(mixed_low, "group", axis=0, tiled=True),
    )
    gate_rows, lift_rows, hidden_rows = (
        lax.all_gather(grad_gate_low, "group", axis=0, tiled=True),
        lax.all_gather(grad_lift_low, "group", axis=0, tiled=True),
        lax.all_gather(hidden, "group", axis=0, tiled=True),
    )
    partial_sums = (
        inner_t(normed_own, query_rows),
        inner_t(normed_own, key_rows),
        inner_t(normed_own, value_rows),
        inner_t(middle_own, mixed_rows),
        inner_t(normed_mlp_own, gate_rows),
        inner_t(normed_mlp_own, lift_rows),
        inner_t(top_own, hidden_rows),
    )
    grad_query, grad_key, grad_value, grad_out, grad_gate, grad_up, grad_down = (
        lax.psum_scatter(
            partial_sums[0].astype(jnp.bfloat16), "replica", scatter_dimension=0, tiled=True
        ).astype(jnp.float32),
        lax.psum_scatter(
            partial_sums[1].astype(jnp.bfloat16), "replica", scatter_dimension=0, tiled=True
        ).astype(jnp.float32),
        lax.psum_scatter(
            partial_sums[2].astype(jnp.bfloat16), "replica", scatter_dimension=0, tiled=True
        ).astype(jnp.float32),
        lax.psum_scatter(
            partial_sums[3].astype(jnp.bfloat16), "replica", scatter_dimension=0, tiled=True
        ).astype(jnp.float32),
        lax.psum_scatter(
            partial_sums[4].astype(jnp.bfloat16), "replica", scatter_dimension=0, tiled=True
        ).astype(jnp.float32),
        lax.psum_scatter(
            partial_sums[5].astype(jnp.bfloat16), "replica", scatter_dimension=0, tiled=True
        ).astype(jnp.float32),
        lax.psum_scatter(
            partial_sums[6].astype(jnp.bfloat16), "replica", scatter_dimension=0, tiled=True
        ).astype(jnp.float32),
    )
    gain_owned = lax.psum_scatter(
        jnp.stack([grad_gain_one, grad_gain_two]),
        ("group", "replica"),
        scatter_dimension=1,
        tiled=True,
    )
    squares = jnp.stack(
        [
            jnp.sum((source * source).reshape(sequences, -1), axis=1),
            jnp.sum((middle * middle).reshape(sequences, -1), axis=1),
            jnp.sum((output_full * output_full).reshape(sequences, -1), axis=1),
        ],
        axis=1,
    )
    square_totals = lax.psum(squares, "group")
    stream_rms = jnp.sqrt(square_totals / (full_len * model_width))
    layer_out = output_full.astype(jnp.bfloat16).reshape(sequences, block_size, model_width)
    input_grad = input_grad.reshape(sequences, block_size, model_width)
    return (
        layer_out,
        input_grad,
        gain_owned[0],
        grad_query,
        grad_key,
        grad_value,
        grad_out,
        gain_owned[1],
        grad_gate,
        grad_up,
        grad_down,
        stream_rms,
    )


def solution(mesh):
    placed = (
        P("replica", "group", None),
        P("replica", "group"),
        P("replica", None),
        P("group"),
        P("group", None),
        P("group", None),
        P("group", None),
        P("group", None),
        P("group"),
        P("group", None),
        P("group", None),
        P("group", None),
        P("replica", "group", None),
    )
    return jax.shard_map(
        shards,
        mesh=mesh,
        in_specs=placed,
        out_specs=(
            P("replica", "group", None),
            P("replica", "group", None),
            P(("group", "replica")),
            P(("group", "replica"), None),
            P(("group", "replica"), None),
            P(("group", "replica"), None),
            P(("group", "replica"), None),
            P(("group", "replica")),
            P(("group", "replica"), None),
            P(("group", "replica"), None),
            P(("group", "replica"), None),
            P("replica", None),
        ),
        check_vma=False,
    )
```

profile of v0, /device:TPU:0, one launch (start us, length us, event | category | flops | bytes accessed | tf_op | source)
XLA Modules:
  0.0 4407.7 jit_solution(10174914001787924033)
XLA Ops:
  9.4 14.6 all-gather.3
  27.3 50.7 %all-gather.24.cloned.1.call-done = bf16[2560,640]{1,0:T(8,128)(2,1)} async-done(((bf16[640,640]{1,0:T(8,128)(2,1)}), bf16[2560,640]{1,0:T(8,128)(2,1)}) %all-gather.24.cloned.1.call-update) | async-done | bytes 3276816 | tf_op jit(solution)/shard_map/all_gather | solution.py:91
  86.8 57.1 %all-gather.22.cloned.1.call-done = bf16[2560,640]{1,0:T(8,128)(2,1)} async-done(((bf16[640,640]{1,0:T(8,128)(2,1)}), bf16[2560,640]{1,0:T(8,128)(2,1)}) %all-gather.22.cloned.1.call-update) | async-done | bytes 3276816 | tf_op jit(solution)/shard_map/all_gather | solution.py:92
  153.2 13.6 all-gather.4
  179.2 32.1 all-gather.48.cloned.1.call-done
  213.7 224.8 %all-gather.26.cloned.1.call-done = bf16[2560,2560]{1,0:T(8,128)(2,1)} async-done(((bf16[640,2560]{1,0:T(8,128)(2,1)}), bf16[2560,2560]{1,0:T(8,128)(2,1)}) %all-gather.26.cloned.1.call-update) | async-done | bytes 13107216 | tf_op jit(solution)/shard_map/all_gather | solution.py:90
  438.5 8.5 fusion.39
  447.7 14.4 fusion.49
  462.2 13.2 fusion.3
  475.4 13.8 fusion.28
  489.3 175.7 %all-gather.28.cloned.1.call-done = bf16[2560,2560]{1,0:T(8,128)(2,1)} async-done(((bf16[640,2560]{1,0:T(8,128)(2,1)}), bf16[2560,2560]{1,0:T(8,128)(2,1)}) %all-gather.28.cloned.1.call-update) | async-done | bytes 13107216 | tf_op jit(solution)/shard_map/all_gather | solution.py:93
  673.9 605.2 %all-gather.30.cloned.1.call-done = bf16[2560,7168]{1,0:T(8,128)(2,1)} async-done(((bf16[640,7168]{1,0:T(8,128)(2,1)}), bf16[2560,7168]{1,0:T(8,128)(2,1)}) %all-gather.30.cloned.1.call-update) | async-done | bytes 36700176 | tf_op jit(solution)/shard_map/all_gather | solution.py:162
  1279.1 24.5 fusion.50
  1303.6 590.1 %all-gather.32.cloned.1.call-done = bf16[2560,7168]{1,0:T(8,128)(2,1)} async-done(((bf16[640,7168]{1,0:T(8,128)(2,1)}), bf16[2560,7168]{1,0:T(8,128)(2,1)}) %all-gather.32.cloned.1.call-update) | async-done | bytes 36700176 | tf_op jit(solution)/shard_map/all_gather | solution.py:163
  1893.7 24.5 fusion.51
  1918.3 590.1 %all-gather.34.cloned.1.call-done = bf16[2560,7168]{1,0:T(8,128)(2,1)} async-done(((bf16[640,7168]{1,0:T(8,128)(2,1)}), bf16[2560,7168]{1,0:T(8,128)(2,1)}) %all-gather.34.cloned.1.call-update) | async-done | bytes 36700176 | tf_op jit(solution)/shard_map/all_gather | solution.py:164
  2508.4 27.7 multiply_convert_fusion
  2536.1 18.5 fusion.52
  2554.6 21.0 multiply_reduce_fusion.1
  2590.0 14.7 fusion.5
  2606.1 22.3 fusion
  2628.4 28.1 fusion.2
  2656.5 12.5 bitcast_multiply_fusion.3
  2671.6 48.2 %reduce-scatter.15.cloned.1.call-done = f32[1,256,640]{1,2,0:T(8,128)} async-done(((f32[1,1024,640]{1,2,0:T(8,128)}), f32[1,256,640]{1,2,0:T(8,128)}) %reduce-scatter.15.cloned.1.call-update) | async-done | bytes 655376 | tf_op jit(solution)/shard_map/reduce_scatter | solution.py:247
  2722.5 9.0 convolution_multiply_fusion
  2756.1 91.9 %all-gather.40.cloned.1.call-done = bf16[1024,2560]{0,1:T(8,128)(2,1)} async-done(((bf16[256,2560]{0,1:T(8,128)(2,1)}), bf16[1024,2560]{0,1:T(8,128)(2,1)}) %all-gather.40.cloned.1.call-update) | async-done | bytes 5242896 | tf_op jit(solution)/shard_map/all_gather | solution.py:279
  2861.0 51.0 %all_to_all.73 = bf16[256,4,640]{2,0,1:T(8,128)(2,1)S(1)} all-to-all(bf16[256,4,640]{2,0,1:T(8,128)(2,1)S(1)} %fusion.27), channel_id=1, replica_groups=mesh['group'=4,'replica'=8] {'group'}, dimensions={1} | all-to-all | bytes 2621440 | tf_op jit(solution)/shard_map/all_to_all | solution.py:270
  2915.5 24.7 all-gather.38.cloned.1.call-done
  2943.8 94.7 %all-gather.36.cloned.1.call-done = bf16[1024,2560]{0,1:T(8,128)(2,1)} async-done(((bf16[256,2560]{0,1:T(8,128)(2,1)}), bf16[1024,2560]{0,1:T(8,128)(2,1)}) %all-gather.36.cloned.1.call-update) | async-done | bytes 5242896 | tf_op jit(solution)/shard_map/all_gather | solution.py:276
  3049.3 76.3 %all_to_all.74 = bf16[256,4,640]{0,2,1:T(8,128)(2,1)S(1)} all-to-all(bf16[256,4,640]{0,2,1:T(8,128)(2,1)} %bitcast.221), channel_id=1, replica_groups=mesh['group'=4,'replica'=8] {'group'}, dimensions={1} | all-to-all | bytes 2621440 | tf_op jit(solution)/shard_map/all_to_all | solution.py:273
  3127.0 191.6 %all-gather.46.cloned.1.call-done = bf16[1024,7168]{1,0:T(8,128)(2,1)} async-done(((bf16[256,7168]{1,0:T(8,128)(2,1)}), bf16[1024,7168]{1,0:T(8,128)(2,1)}) %all-gather.46.cloned.1.call-update) | async-done | bytes 14680080 | tf_op jit(solution)/shard_map/all_gather | solution.py:284
  3318.6 17.5 fusion.9
  3336.1 12.9 copy.109
  3350.5 75.0 %all_to_all.75 = bf16[256,4,640]{2,0,1:T(8,128)(2,1)S(1)} all-to-all(bf16[256,4,640]{2,0,1:T(8,128)(2,1)S(1)} %bitcast.220), channel_id=1, replica_groups=mesh['group'=4,'replica'=8] {'group'}, dimensions={1} | all-to-all | bytes 2621440 | tf_op jit(solution)/shard_map/all_to_all | solution.py:272
  3425.5 173.3 %all-gather.42.cloned.1.call-done = bf16[1024,7168]{1,0:T(8,128)(2,1)} async-done(((bf16[256,7168]{1,0:T(8,128)(2,1)}), bf16[1024,7168]{1,0:T(8,128)(2,1)}) %all-gather.42.cloned.1.call-update) | async-done | bytes 14680080 | tf_op jit(solution)/shard_map/all_gather | solution.py:282
  3598.7 17.4 convolution_convert_fusion.1
  3616.4 234.5 %all-gather.44.cloned.1.call-done = bf16[1024,7168]{1,0:T(8,128)(2,1)} async-done(((bf16[256,7168]{1,0:T(8,128)(2,1)}), bf16[1024,7168]{1,0:T(8,128)(2,1)}) %all-gather.44.cloned.1.call-update) | async-done | bytes 14680080 | tf_op jit(solution)/shard_map/all_gather | solution.py:283
  3850.8 17.4 convolution_convert_fusion
  3869.5 20.0 multiply_reduce_fusion
  3891.5 8.6 psum.7
  3905.4 81.6 %reduce-scatter.31.cloned.1.call-done = f32[80,2]{1,0:T(8,128)} async-done(((f32[2560,2]{1,0:T(8,128)}), f32[80,2]{1,0:T(8,128)}) %reduce-scatter.31.cloned.1.call-update) | async-done | bytes 656
  3989.1 44.5 %reduce-scatter.25.cloned.1.call-done = bf16[80,2560]{1,0:T(8,128)(2,1)} async-done(((bf16[640,2560]{1,0:T(8,128)(2,1)}), bf16[80,2560]{1,0:T(8,128)(2,1)}) %reduce-scatter.25.cloned.1.call-update) | async-done | bytes 409616 | tf_op jit(solution)/shard_map/reduce_scatter | solution.py:305
  4035.5 36.8 reduce-scatter.23.cloned.1.call-done
  4073.9 36.8 reduce-scatter.21.cloned.1.call-done
  4112.4 49.1 %reduce-scatter.19.cloned.1.call-done = bf16[80,2560]{1,0:T(8,128)(2,1)} async-done(((bf16[640,2560]{1,0:T(8,128)(2,1)}), bf16[80,2560]{1,0:T(8,128)(2,1)}) %reduce-scatter.19.cloned.1.call-update) | async-done | bytes 409616 | tf_op jit(solution)/shard_map/reduce_scatter | solution.py:296
  4163.4 77.1 %reduce-scatter.33.cloned.1.call-done = bf16[80,7168]{1,0:T(8,128)(2,1)} async-done(((bf16[640,7168]{1,0:T(8,128)(2,1)}), bf16[80,7168]{1,0:T(8,128)(2,1)}) %reduce-scatter.33.cloned.1.call-update) | async-done | bytes 1146896
  4244.3 74.9 %reduce-scatter.27.cloned.1.call-done = bf16[80,7168]{1,0:T(8,128)(2,1)} async-done(((bf16[640,7168]{1,0:T(8,128)(2,1)}), bf16[80,7168]{1,0:T(8,128)(2,1)}) %reduce-scatter.27.cloned.1.call-update) | async-done | bytes 1146896 | tf_op jit(solution)/shard_map/reduce_scatter | solution.py:308
  4322.0 76.2 %reduce-scatter.29.cloned.1.call-done = bf16[80,7168]{1,0:T(8,128)(2,1)} async-done(((bf16[640,7168]{1,0:T(8,128)(2,1)}), bf16[80,7168]{1,0:T(8,128)(2,1)}) %reduce-scatter.29.cloned.1.call-update) | async-done | bytes 1146896 | tf_op jit(solution)/shard_map/reduce_scatter | solution.py:311
  (212 shorter events, 152.8 us)
Async XLA Ops:
  7.2 70.8 %all-gather.24.cloned.1.call-start = ((), (), s32[]{:S(2)}) async-start(), calls=%async_computation.15 | async-start | bytes 4096000 | tf_op jit(solution)/shard_map/all_gather | solution.py:91
  7.9 18.5 copy-start
  7.9 135.9 %all-gather.22.cloned.1.call-start = ((), (), s32[]{:S(2)}) async-start(), calls=%async_computation.14 | async-start | bytes 4096000 | tf_op jit(solution)/shard_map/all_gather | solution.py:92
  8.7 168.9 %all-gather.50.cloned.1.call-start = ((), (), s32[]{:S(2)}) async-start(), calls=%async_computation.36 | async-start | bytes 1638400 | tf_op jit(solution)/shard_map/all_gather | solution.py:121
  24.7 413.8 %copy-start.27 = (f32[2560]{0:T(1024)}, f32[2560]{0:T(1024)S(1)}, u32[]{:S(2)}) copy-start(f32[2560]{0:T(1024)S(1)} %reshape.535) | copy-start | bytes 30724
  25.8 421.4 %copy-start.22 = (f32[256,80]{0,1:T(8,128)}, f32[256,80]{0,1:T(8,128)S(1)}, u32[]{:S(2)}) copy-start(f32[256,80]{0,1:T(8,128)S(1)} %get-tuple-element.147) | copy-start | bytes 245764
  25.8 421.4 %copy-start.24 = (f32[256,80]{0,1:T(8,128)}, f32[256,80]{0,1:T(8,128)S(1)}, u32[]{:S(2)}) copy-start(f32[256,80]{0,1:T(8,128)S(1)} %get-tuple-element.148) | copy-start | bytes 245764
  27.3 411.2 %copy-start.31 = (f32[256]{0:T(256)}, f32[256]{0:T(256)S(1)}, u32[]{:S(2)}) copy-start(f32[256]{0:T(256)S(1)} %get-tuple-element.150) | copy-start | bytes 3076
  86.8 124.5 %all-gather.48.cloned.1.call-start = ((), (), s32[]{:S(2)}) async-start(), calls=%async_computation.35 | async-start | bytes 1638400 | tf_op jit(solution)/shard_map/all_gather | solution.py:122
  147.8 290.7 %all-gather.26.cloned.1.call-start = ((), (), s32[]{:S(2)}) async-start(), calls=%async_computation.16 | async-start | bytes 16384000 | tf_op jit(solution)/shard_map/all_gather | solution.py:90
  148.4 516.5 %all-gather.28.cloned.1.call-start = ((), (), s32[]{:S(2)}) async-start(), calls=%async_computation.17 | async-start | bytes 16384000 | tf_op jit(solution)/shard_map/all_gather | solution.py:93
  149.0 1130.1 %all-gather.30.cloned.1.call-start = ((), (), s32[]{:S(2)}) async-start(), calls=%async_computation.18 | async-start | bytes 45875200 | tf_op jit(solution)/shard_map/all_gather | solution.py:162
  149.7 1744.0 %all-gather.32.cloned.1.call-start = ((), (), s32[]{:S(2)}) async-start(), calls=%async_computation.19 | async-start | bytes 45875200 | tf_op jit(solution)/shard_map/all_gather | solution.py:163
  150.5 2.7 copy-start.34
  150.5 2357.9 %all-gather.34.cloned.1.call-start = ((), (), s32[]{:S(2)}) async-start(), calls=%async_computation.20 | async-start | bytes 45875200 | tf_op jit(solution)/shard_map/all_gather | solution.py:164
  151.2 2518.5 %reduce-scatter.17.cloned.1.call-start = ((), (), s32[]{:S(2)}) async-start(), calls=%async_computation.22 | async-start | bytes 3276800 | tf_op jit(solution)/shard_map/reduce_scatter | solution.py:248
  179.2 268.6 %copy-start.4 = (bf16[1024,640]{0,1:T(8,128)(2,1)}, bf16[1024,640]{0,1:T(8,128)(2,1)S(1)}, u32[]{:S(2)}) copy-start(bf16[1024,640]{0,1:T(8,128)(2,1)S(1)} %copy.84) | copy-start | bytes 3932164
  447.7 14.4 copy-start.2
  462.1 13.3 copy-start.8
  489.2 182.7 %copy-start.26 = (bf16[8,80,4,256]{3,1,2,0:T(8,128)(2,1)}, bf16[8,80,4,256]{3,1,2,0:T(8,128)(2,1)S(1)}, u32[]{:S(2)}) copy-start(bf16[8,80,4,256]{3,1,2,0:T(8,128)(2,1)S(1)} %fusion.28) | copy-start | bytes 3932164
  673.9 1219.8 %copy-start.12 = (bf16[256,2560]{1,0:T(8,128)(2,1)}, bf16[256,2560]{1,0:T(8,128)(2,1)S(1)}, u32[]{:S(2)}) copy-start(bf16[256,2560]{1,0:T(8,128)(2,1)S(1)} %multiply_convert_fusion.3) | copy-start | bytes 3932164
  1303.6 1204.8 %copy-start.10 = (bf16[1,256,2560]{2,1,0:T(8,128)(2,1)S(1)}, bf16[1,256,2560]{2,1,0:T(8,128)(2,1)}, u32[]{:S(2)}) copy-start(bf16[1,256,2560]{2,1,0:T(8,128)(2,1)} %param.25) | copy-start | bytes 3932164
  2536.1 18.5 copy-start.7
  2604.8 115.0 %reduce-scatter.15.cloned.1.call-start = ((), (), s32[]{:S(2)}) async-start(), calls=%async_computation.21 | async-start | bytes 3276800 | tf_op jit(solution)/shard_map/reduce_scatter | solution.py:247
  2628.4 28.1 copy-start.3
  2669.0 50.8 %copy-start.25 = (f32[256,80]{0,1:T(8,128)S(1)}, f32[256,80]{0,1:T(8,128)}, u32[]{:S(2)}) copy-start(f32[256,80]{0,1:T(8,128)} %copy-done.24) | copy-start | bytes 245764
  2669.0 178.9 %all-gather.40.cloned.1.call-start = ((), (), s32[]{:S(2)}) async-start(), calls=%async_computation.28 | async-start | bytes 6553600 | tf_op jit(solution)/shard_map/all_gather | solution.py:279
  2669.6 51.5 %copy-start.23 = (f32[256,80]{0,1:T(8,128)S(1)}, f32[256,80]{0,1:T(8,128)}, u32[]{:S(2)}) copy-start(f32[256,80]{0,1:T(8,128)} %copy-done.22) | copy-start | bytes 245764
  2669.6 242.4 %all-gather.52.cloned.1.call-start = ((), (), s32[]{:S(2)}) async-start(), calls=%async_computation.37 | async-start | bytes 1638400 | tf_op jit(solution)/shard_map/all_gather | solution.py:278
  2671.6 268.7 %all-gather.38.cloned.1.call-start = ((), (), s32[]{:S(2)}) async-start(), calls=%async_computation.25 | async-start | bytes 1638400 | tf_op jit(solution)/shard_map/all_gather | solution.py:277
  2722.0 316.5 %all-gather.36.cloned.1.call-start = ((), (), s32[]{:S(2)}) async-start(), calls=%async_computation.23 | async-start | bytes 6553600 | tf_op jit(solution)/shard_map/all_gather | solution.py:276
  2733.8 584.8 %all-gather.46.cloned.1.call-start = ((), (), s32[]{:S(2)}) async-start(), calls=%async_computation.34 | async-start | bytes 18350080 | tf_op jit(solution)/shard_map/all_gather | solution.py:284
  2734.4 864.3 %all-gather.42.cloned.1.call-start = ((), (), s32[]{:S(2)}) async-start(), calls=%async_computation.30 | async-start | bytes 18350080 | tf_op jit(solution)/shard_map/all_gather | solution.py:282
  2735.0 1115.8 %all-gather.44.cloned.1.call-start = ((), (), s32[]{:S(2)}) async-start(), calls=%async_computation.32 | async-start | bytes 18350080 | tf_op jit(solution)/shard_map/all_gather | solution.py:283
  2736.3 5.6 copy-start.16
  2737.5 110.5 %all-to-all-start.1 = ((bf16[256,4,640]{2,0,1:T(8,128)(2,1)}), bf16[256,4,640]{2,0,1:T(8,128)(2,1)}, u32[]{:S(2)}, u32[]{:S(2)}) async-start(bf16[256,4,640]{2,0,1:T(8,128)(2,1)} %bitcast.218), calls=%async_computation.6 | async-start | bytes 2621440 | tf_op jit(solution)/shard_map/all_to_all | solution.py:271
  2741.8 7.0 copy-start.20
  2741.8 1245.2 %reduce-scatter.31.cloned.1.call-start = ((), (), s32[]{:S(2)}) async-start(), calls=%async_computation.38 | async-start | bytes 1351680
  2741.9 6.9 copy-start.17
  2748.8 2.3 copy-start.19
  2755.8 1277.8 %reduce-scatter.25.cloned.1.call-start = ((), (), s32[]{:S(2)}) async-start(), calls=%async_computation.29 | async-start | bytes 3686400 | tf_op jit(solution)/shard_map/reduce_scatter | solution.py:305
  2856.2 1216.2 %reduce-scatter.23.cloned.1.call-start = ((), (), s32[]{:S(2)}) async-start(), calls=%async_computation.27 | async-start | bytes 921600 | tf_op jit(solution)/shard_map/reduce_scatter | solution.py:302
  2915.5 1195.3 %reduce-scatter.21.cloned.1.call-start = ((), (), s32[]{:S(2)}) async-start(), calls=%async_computation.26 | async-start | bytes 921600 | tf_op jit(solution)/shard_map/reduce_scatter | solution.py:299
  2943.7 1217.8 %reduce-scatter.19.cloned.1.call-start = ((), (), s32[]{:S(2)}) async-start(), calls=%async_computation.24 | async-start | bytes 3686400 | tf_op jit(solution)/shard_map/reduce_scatter | solution.py:296
  3046.4 1194.1 %reduce-scatter.33.cloned.1.call-start = ((), (), s32[]{:S(2)}) async-start(), calls=%async_computation.39 | async-start | bytes 10321920
  3349.1 970.1 %reduce-scatter.27.cloned.1.call-start = ((), (), s32[]{:S(2)}) async-start(), calls=%async_computation.31 | async-start | bytes 10321920 | tf_op jit(solution)/shard_map/reduce_scatter | solution.py:308
  3616.1 782.0 %reduce-scatter.29.cloned.1.call-start = ((), (), s32[]{:S(2)}) async-start(), calls=%async_computation.33 | async-start | bytes 10321920 | tf_op jit(solution)/shard_map/reduce_scatter | solution.py:311
  3869.5 31.1 copy-start.33
  (15 other events, 21.4 us)
Sparse Core Ops, SparseCore 0:
  9.6 68.3 all-gather.23
  79.5 64.2 all-gather.21
  146.0 31.4 all-gather.49
  179.5 31.6 all-gather.47
  212.7 225.7 all-gather.25
  439.9 224.9 all-gather.27
  666.5 612.5 all-gather.29
  1280.6 613.0 all-gather.31
  1895.3 613.0 all-gather.33
  2604.9 50.8 reduce-scatter.16
  2669.2 50.5 reduce-scatter.14
  2721.2 126.6 all-gather.39
  2850.1 56.3 all-gather.51
  2908.5 31.7 all-gather.37
  2942.2 96.2 all-gather.35
  3039.9 278.6 all-gather.45
  3320.1 278.6 all-gather.41
  3600.2 250.6 all-gather.43
  3853.6 133.3 reduce-scatter.30
  3990.7 42.8 reduce-scatter.24
  4037.8 34.4 reduce-scatter.22
  4076.3 34.4 reduce-scatter.20
  4114.6 46.8 reduce-scatter.18
  4165.4 75.0 reduce-scatter.32
  4244.1 75.0 reduce-scatter.26
  4323.1 75.0 reduce-scatter.28
where the time goes:
time: 4410 us
  waiting for transfers between devices  3680 us (83%)
  matrix products  341 us (8%)
  blocking collectives  239 us (5%)
  other arithmetic  83.8 us (2%)
  local copies, waits for them, and re-layouts  45.3 us (1%)
    all_gather x1, waiting for transfers between devices, shards(): gate_piece = lax.all_gather(w_gate, 'group', axis=0, tiled=True)  605 us
    all_gather x1, waiting for transfers between devices, shards(): down_piece = lax.all_gather(w_down, 'group', axis=0, tiled=True)  590 us
    all_gather x1, waiting for transfers between devices, shards(): up_piece = lax.all_gather(w_up, 'group', axis=0, tiled=True)  590 us
    all_gather x1, waiting for transfers between devices, shards(): lax.all_gather(grad_lift_low, 'group', axis=0, tiled=True)  234 us
    all_gather x1, waiting for transfers between devices, shards(): query_piece = lax.all_gather(w_query, 'group', axis=0, tiled=True)  225 us
    all_gather x1, waiting for transfers between devices, shards(): lax.all_gather(hidden, 'group', axis=0, tiled=True)  192 us
    all_gather x1, waiting for transfers between devices, shards(): out_piece = lax.all_gather(w_out, 'group', axis=0, tiled=True)  176 us
    all_gather x1, waiting for transfers between devices, shards(): lax.all_gather(grad_gate_low, 'group', axis=0, tiled=True)  173 us
  transfers between devices with their start and end apart: 27, of which 24 were waited for; matrix products, arithmetic and copies ran while one was open for 8% of the time, Pallas kernels for 0%

commit v1 on v0

--- a/solution.py
+++ b/solution.py
@@ -160,8 +160,15 @@
     unit_two = middle * inverse_two
     gain_piece = lax.all_gather(gain_mlp, "group", axis=0, tiled=True)
     gate_piece = lax.all_gather(w_gate, "group", axis=0, tiled=True)
-    up_piece = lax.all_gather(w_up, "group", axis=0, tiled=True)
-    down_piece = lax.all_gather(w_down, "group", axis=0, tiled=True)
+
+    def lead_turns(sheet, x0, net_axis):
+        return jnp.split(
+            jax.lax.all_gather(jnp.concatenate([sheet, x0], 1), net_axis, axis=0, tiled=True),
+            [sheet.shape[1]],
+            1,
+        )
+
+    up_piece, down_piece = lead_turns(w_up, w_down, "group")
     scaled = unit_two * gain_piece.astype(jnp.float32)
     scaled = scaled.astype(jnp.bfloat16)
     gated = jnp.dot(scaled, gate_piece, preferred_element_type=jnp.float32)

time: 4410 us -> 4970 us (1.13)
  waiting for transfers between devices: 3680 us -> 4210 us
    all_gather x1, waiting for transfers between devices: 590 us -> 1190 us  [lead_turns(): jax.lax.all_gather(jnp.concatenate([sheet, x0], 1), net_axis, axis=0, til...]
  transfers between devices with their start and end apart: 27 -> 27, of which waited for: 24 -> 23; matrix products, arithmetic and copies ran while one was open for 8% -> 9% of each run, Pallas kernels for 0% -> 0%
where the time goes in v1:
time: 4970 us; the launch traced here: 4960 us
  waiting for transfers between devices  4210 us (85%)
  matrix products  341 us (7%)
  blocking collectives  239 us (5%)
  other arithmetic  99.9 us (2%)
    all_gather x1, waiting for transfers between devices, lead_turns(): jax.lax.all_gather(jnp.concatenate([sheet, x0], 1), net_axis, axis=0, til...  1190 us
    all_gather x1, waiting for transfers between devices, shards(): gate_piece = lax.all_gather(w_gate, 'group', axis=0, tiled=True)  605 us
    all_gather x1, waiting for transfers between devices, shards(): up_piece = lax.all_gather(w_up, 'group', axis=0, tiled=True)  547 us
    all_gather x1, waiting for transfers between devices, shards(): lax.all_gather(grad_lift_low, 'group', axis=0, tiled=True)  234 us
    all_gather x1, waiting for transfers between devices, shards(): query_piece = lax.all_gather(w_query, 'group', axis=0, tiled=True)  225 us
    all_gather x1, waiting for transfers between devices, shards(): lax.all_gather(hidden, 'group', axis=0, tiled=True)  192 us
    all_gather x1, waiting for transfers between devices, shards(): out_piece = lax.all_gather(w_out, 'group', axis=0, tiled=True)  176 us
    all_gather x1, waiting for transfers between devices, shards(): lax.all_gather(grad_gate_low, 'group', axis=0, tiled=True)  173 us
  transfers between devices with their start and end apart: 27, of which 23 were waited for; matrix products, arithmetic and copies ran while one was open for 9% of the time, Pallas kernels for 0%

profile of v1, /device:TPU:0, one launch (start us, length us, event | category | flops | bytes accessed | tf_op | source)
XLA Modules:
  0.0 4961.3 jit_solution(207737675268706585)
XLA Ops:
  9.4 14.6 all-gather.3
  27.3 50.7 %all-gather.24.cloned.1.call-done = bf16[2560,640]{1,0:T(8,128)(2,1)} async-done(((bf16[640,640]{1,0:T(8,128)(2,1)}), bf16[2560,640]{1,0:T(8,128)(2,1)}) %all-gather.24.cloned.1.call-update) | async-done | bytes 3276816 | tf_op jit(solution)/shard_map/all_gather | solution.py:91
  86.8 57.1 %all-gather.22.cloned.1.call-done = bf16[2560,640]{1,0:T(8,128)(2,1)} async-done(((bf16[640,640]{1,0:T(8,128)(2,1)}), bf16[2560,640]{1,0:T(8,128)(2,1)}) %all-gather.22.cloned.1.call-update) | async-done | bytes 3276816 | tf_op jit(solution)/shard_map/all_gather | solution.py:92
  149.8 16.1 pad_maximum_fusion
  168.6 13.1 all-gather.4
  186.5 24.8 all-gather.48.cloned.1.call-done
  213.7 224.8 %all-gather.26.cloned.1.call-done = bf16[2560,2560]{1,0:T(8,128)(2,1)} async-done(((bf16[640,2560]{1,0:T(8,128)(2,1)}), bf16[2560,2560]{1,0:T(8,128)(2,1)}) %all-gather.26.cloned.1.call-update) | async-done | bytes 13107216 | tf_op jit(solution)/shard_map/all_gather | solution.py:90
  447.7 14.4 fusion.60
  462.2 13.2 fusion.9
  475.4 13.8 fusion.40
  489.3 175.6 %all-gather.28.cloned.1.call-done = bf16[2560,2560]{1,0:T(8,128)(2,1)} async-done(((bf16[640,2560]{1,0:T(8,128)(2,1)}), bf16[2560,2560]{1,0:T(8,128)(2,1)}) %all-gather.28.cloned.1.call-update) | async-done | bytes 13107216 | tf_op jit(solution)/shard_map/all_gather | solution.py:93
  673.9 605.1 %all-gather.30.cloned.1.call-done = bf16[2560,7168]{1,0:T(8,128)(2,1)} async-done(((bf16[640,7168]{1,0:T(8,128)(2,1)}), bf16[2560,7168]{1,0:T(8,128)(2,1)}) %all-gather.30.cloned.1.call-update) | async-done | bytes 36700176 | tf_op jit(solution)/shard_map/all_gather | solution.py:162
  1279.0 26.7 fusion.63
  1305.7 1188.6 %all-gather.32.cloned.1.call-done = bf16[2560,14336]{1,0:T(8,128)(2,1)} async-done(((bf16[640,14336]{1,0:T(8,128)(2,1)}), bf16[2560,14336]{1,0:T(8,128)(2,1)}) %all-gather.32.cloned.1.call-update) | async-done | bytes 73400336 | tf_op jit(solution)/shard_map/all_gather | solution.py:166
  2494.3 23.2 fusion
  2517.5 25.2 multiply_convert_fusion
  2542.7 19.2 fusion.64
  2561.9 546.6 %all-gather.34.cloned.1.call-done = bf16[2560,7168]{1,0:T(8,128)(2,1)} async-done(((bf16[640,7168]{1,0:T(8,128)(2,1)}), bf16[2560,7168]{1,0:T(8,128)(2,1)}) %all-gather.34.cloned.1.call-update) | async-done | bytes 36700176 | tf_op jit(solution)/shard_map/all_gather | solution.py:193
  3108.6 20.6 multiply_reduce_fusion.1
  3143.6 14.9 fusion.11
  3159.8 22.2 fusion.2
  3182.1 28.1 fusion.4
  3210.2 12.6 bitcast_multiply_fusion.3
  3225.4 48.2 reduce-scatter.15.cloned.1.call-done
  3276.2 9.1 convolution_multiply_fusion
  3310.1 91.6 %all-gather.40.cloned.1.call-done = bf16[1024,2560]{0,1:T(8,128)(2,1)} async-done(((bf16[256,2560]{0,1:T(8,128)(2,1)}), bf16[1024,2560]{0,1:T(8,128)(2,1)}) %all-gather.40.cloned.1.call-update) | async-done | bytes 5242896 | tf_op jit(solution)/shard_map/all_gather | solution.py:286
  3414.7 50.8 %all_to_all.73 = bf16[256,4,640]{2,0,1:T(8,128)(2,1)S(1)} all-to-all(bf16[256,4,640]{2,0,1:T(8,128)(2,1)S(1)} %fusion.39), channel_id=1, replica_groups=mesh['group'=4,'replica'=8] {'group'}, dimensions={1} | all-to-all | bytes 2621440 | tf_op jit(solution)/shard_map/all_to_all | solution.py:277
  3469.2 24.5 all-gather.38.cloned.1.call-done
  3497.3 94.7 %all-gather.36.cloned.1.call-done = bf16[1024,2560]{0,1:T(8,128)(2,1)} async-done(((bf16[256,2560]{0,1:T(8,128)(2,1)}), bf16[1024,2560]{0,1:T(8,128)(2,1)}) %all-gather.36.cloned.1.call-update) | async-done | bytes 5242896 | tf_op jit(solution)/shard_map/all_gather | solution.py:283
  3602.8 76.3 %all_to_all.74 = bf16[256,4,640]{0,2,1:T(8,128)(2,1)S(1)} all-to-all(bf16[256,4,640]{0,2,1:T(8,128)(2,1)} %bitcast.220), channel_id=1, replica_groups=mesh['group'=4,'replica'=8] {'group'}, dimensions={1} | all-to-all | bytes 2621440 | tf_op jit(solution)/shard_map/all_to_all | solution.py:280
  3680.5 191.6 %all-gather.46.cloned.1.call-done = bf16[1024,7168]{1,0:T(8,128)(2,1)} async-done(((bf16[256,7168]{1,0:T(8,128)(2,1)}), bf16[1024,7168]{1,0:T(8,128)(2,1)}) %all-gather.46.cloned.1.call-update) | async-done | bytes 14680080 | tf_op jit(solution)/shard_map/all_gather | solution.py:291
  3872.1 17.5 fusion.15
  3889.6 12.9 copy.114
  3903.9 75.0 %all_to_all.75 = bf16[256,4,640]{2,0,1:T(8,128)(2,1)S(1)} all-to-all(bf16[256,4,640]{2,0,1:T(8,128)(2,1)S(1)} %bitcast.219), channel_id=1, replica_groups=mesh['group'=4,'replica'=8] {'group'}, dimensions={1} | all-to-all | bytes 2621440 | tf_op jit(solution)/shard_map/all_to_all | solution.py:279
  3978.9 173.3 %all-gather.42.cloned.1.call-done = bf16[1024,7168]{1,0:T(8,128)(2,1)} async-done(((bf16[256,7168]{1,0:T(8,128)(2,1)}), bf16[1024,7168]{1,0:T(8,128)(2,1)}) %all-gather.42.cloned.1.call-update) | async-done | bytes 14680080 | tf_op jit(solution)/shard_map/all_gather | solution.py:289
  4152.2 17.4 convolution_convert_fusion.1
  4169.9 234.4 %all-gather.44.cloned.1.call-done = bf16[1024,7168]{1,0:T(8,128)(2,1)} async-done(((bf16[256,7168]{1,0:T(8,128)(2,1)}), bf16[1024,7168]{1,0:T(8,128)(2,1)}) %all-gather.44.cloned.1.call-update) | async-done | bytes 14680080 | tf_op jit(solution)/shard_map/all_gather | solution.py:290
  4404.3 17.4 convolution_convert_fusion
  4423.0 20.2 multiply_reduce_fusion
  4445.2 8.6 psum.7
  4459.1 81.5 %reduce-scatter.31.cloned.1.call-done = f32[80,2]{1,0:T(8,128)} async-done(((f32[2560,2]{1,0:T(8,128)}), f32[80,2]{1,0:T(8,128)}) %reduce-scatter.31.cloned.1.call-update) | async-done | bytes 656
  4542.7 44.4 reduce-scatter.25.cloned.1.call-done
  4589.1 36.8 reduce-scatter.23.cloned.1.call-done
  4627.5 36.8 reduce-scatter.21.cloned.1.call-done
  4665.9 49.1 reduce-scatter.19.cloned.1.call-done
  4717.0 77.1 %reduce-scatter.33.cloned.1.call-done = bf16[80,7168]{1,0:T(8,128)(2,1)} async-done(((bf16[640,7168]{1,0:T(8,128)(2,1)}), bf16[80,7168]{1,0:T(8,128)(2,1)}) %reduce-scatter.33.cloned.1.call-update) | async-done | bytes 1146896
  4797.8 74.9 %reduce-scatter.27.cloned.1.call-done = bf16[80,7168]{1,0:T(8,128)(2,1)} async-done(((bf16[640,7168]{1,0:T(8,128)(2,1)}), bf16[80,7168]{1,0:T(8,128)(2,1)}) %reduce-scatter.27.cloned.1.call-update) | async-done | bytes 1146896 | tf_op jit(solution)/shard_map/reduce_scatter | solution.py:315
  4875.5 76.2 %reduce-scatter.29.cloned.1.call-done = bf16[80,7168]{1,0:T(8,128)(2,1)} async-done(((bf16[640,7168]{1,0:T(8,128)(2,1)}), bf16[80,7168]{1,0:T(8,128)(2,1)}) %reduce-scatter.29.cloned.1.call-update) | async-done | bytes 1146896 | tf_op jit(solution)/shard_map/reduce_scatter | solution.py:318
  (213 shorter events, 153.4 us)
Async XLA Ops:
  7.2 70.8 %all-gather.24.cloned.1.call-start = ((), (), s32[]{:S(2)}) async-start(), calls=%async_computation.15 | async-start | bytes 4096000 | tf_op jit(solution)/shard_map/all_gather | solution.py:91
  7.9 18.5 copy-start
  7.9 136.0 %all-gather.22.cloned.1.call-start = ((), (), s32[]{:S(2)}) async-start(), calls=%async_computation.14 | async-start | bytes 4096000 | tf_op jit(solution)/shard_map/all_gather | solution.py:92
  8.7 176.1 %all-gather.50.cloned.1.call-start = ((), (), s32[]{:S(2)}) async-start(), calls=%async_computation.36 | async-start | bytes 1638400 | tf_op jit(solution)/shard_map/all_gather | solution.py:121
  24.7 413.8 %copy-start.27 = (f32[2560]{0:T(1024)}, f32[2560]{0:T(1024)S(1)}, u32[]{:S(2)}) copy-start(f32[2560]{0:T(1024)S(1)} %reshape.535) | copy-start | bytes 30724
  25.8 421.4 %copy-start.22 = (f32[256,80]{0,1:T(8,128)}, f32[256,80]{0,1:T(8,128)S(1)}, u32[]{:S(2)}) copy-start(f32[256,80]{0,1:T(8,128)S(1)} %get-tuple-element.147) | copy-start | bytes 245764
  25.8 421.4 %copy-start.24 = (f32[256,80]{0,1:T(8,128)}, f32[256,80]{0,1:T(8,128)S(1)}, u32[]{:S(2)}) copy-start(f32[256,80]{0,1:T(8,128)S(1)} %get-tuple-element.148) | copy-start | bytes 245764
  27.3 411.1 %copy-start.31 = (f32[256]{0:T(256)}, f32[256]{0:T(256)S(1)}, u32[]{:S(2)}) copy-start(f32[256]{0:T(256)S(1)} %get-tuple-element.150) | copy-start | bytes 3076
  86.8 124.5 %all-gather.48.cloned.1.call-start = ((), (), s32[]{:S(2)}) async-start(), calls=%async_computation.35 | async-start | bytes 1638400 | tf_op jit(solution)/shard_map/all_gather | solution.py:122
  147.8 290.7 %all-gather.26.cloned.1.call-start = ((), (), s32[]{:S(2)}) async-start(), calls=%async_computation.16 | async-start | bytes 16384000 | tf_op jit(solution)/shard_map/all_gather | solution.py:90
  148.4 516.5 %all-gather.28.cloned.1.call-start = ((), (), s32[]{:S(2)}) async-start(), calls=%async_computation.17 | async-start | bytes 16384000 | tf_op jit(solution)/shard_map/all_gather | solution.py:93
  149.0 1130.1 %all-gather.30.cloned.1.call-start = ((), (), s32[]{:S(2)}) async-start(), calls=%async_computation.18 | async-start | bytes 45875200 | tf_op jit(solution)/shard_map/all_gather | solution.py:162
  149.7 2344.6 %all-gather.32.cloned.1.call-start = ((), (), s32[]{:S(2)}) async-start(), calls=%async_computation.19 | async-start | bytes 91750400 | tf_op jit(solution)/shard_map/all_gather | solution.py:166
  165.9 2.7 copy-start.34
  165.9 2942.7 %all-gather.34.cloned.1.call-start = ((), (), s32[]{:S(2)}) async-start(), calls=%async_computation.20 | async-start | bytes 45875200 | tf_op jit(solution)/shard_map/all_gather | solution.py:193
  166.6 3056.8 %reduce-scatter.17.cloned.1.call-start = ((), (), s32[]{:S(2)}) async-start(), calls=%async_computation.22 | async-start | bytes 3276800 | tf_op jit(solution)/shard_map/reduce_scatter | solution.py:255
  186.5 261.3 %copy-start.4 = (bf16[1024,640]{0,1:T(8,128)(2,1)}, bf16[1024,640]{0,1:T(8,128)(2,1)S(1)}, u32[]{:S(2)}) copy-start(bf16[1024,640]{0,1:T(8,128)(2,1)S(1)} %copy.87) | copy-start | bytes 3932164
  447.7 14.4 copy-start.2
  462.2 13.3 copy-start.8
  489.2 182.7 %copy-start.26 = (bf16[8,80,4,256]{3,1,2,0:T(8,128)(2,1)}, bf16[8,80,4,256]{3,1,2,0:T(8,128)(2,1)S(1)}, u32[]{:S(2)}) copy-start(bf16[8,80,4,256]{3,1,2,0:T(8,128)(2,1)S(1)} %fusion.40) | copy-start | bytes 3932164
  673.9 1820.4 %copy-start.12 = (bf16[256,2560]{1,0:T(8,128)(2,1)}, bf16[256,2560]{1,0:T(8,128)(2,1)S(1)}, u32[]{:S(2)}) copy-start(bf16[256,2560]{1,0:T(8,128)(2,1)S(1)} %multiply_convert_fusion.3) | copy-start | bytes 3932164
  1305.7 1211.8 %copy-start.10 = (bf16[1,256,2560]{2,1,0:T(8,128)(2,1)S(1)}, bf16[1,256,2560]{2,1,0:T(8,128)(2,1)}, u32[]{:S(2)}) copy-start(bf16[1,256,2560]{2,1,0:T(8,128)(2,1)} %param.25) | copy-start | bytes 3932164
  2542.7 565.8 %copy-start.7 = (f32[256,2560]{1,0:T(8,128)S(1)}, f32[256,2560]{1,0:T(8,128)}, u32[]{:S(2)}) copy-start(f32[256,2560]{1,0:T(8,128)} %copy-done.6) | copy-start | bytes 7864324
  3158.5 115.0 %reduce-scatter.15.cloned.1.call-start = ((), (), s32[]{:S(2)}) async-start(), calls=%async_computation.21 | async-start | bytes 3276800 | tf_op jit(solution)/shard_map/reduce_scatter | solution.py:254
  3182.1 28.1 copy-start.3
  3222.8 50.8 %copy-start.25 = (f32[256,80]{0,1:T(8,128)S(1)}, f32[256,80]{0,1:T(8,128)}, u32[]{:S(2)}) copy-start(f32[256,80]{0,1:T(8,128)} %copy-done.24) | copy-start | bytes 245764
  3222.8 178.9 %all-gather.40.cloned.1.call-start = ((), (), s32[]{:S(2)}) async-start(), calls=%async_computation.28 | async-start | bytes 6553600 | tf_op jit(solution)/shard_map/all_gather | solution.py:286
  3223.4 51.5 %copy-start.23 = (f32[256,80]{0,1:T(8,128)S(1)}, f32[256,80]{0,1:T(8,128)}, u32[]{:S(2)}) copy-start(f32[256,80]{0,1:T(8,128)} %copy-done.22) | copy-start | bytes 245764
  3223.4 242.1 %all-gather.52.cloned.1.call-start = ((), (), s32[]{:S(2)}) async-start(), calls=%async_computation.37 | async-start | bytes 1638400 | tf_op jit(solution)/shard_map/all_gather | solution.py:285
  3225.3 268.4 %all-gather.38.cloned.1.call-start = ((), (), s32[]{:S(2)}) async-start(), calls=%async_computation.25 | async-start | bytes 1638400 | tf_op jit(solution)/shard_map/all_gather | solution.py:284
  3275.7 316.2 %all-gather.36.cloned.1.call-start = ((), (), s32[]{:S(2)}) async-start(), calls=%async_computation.23 | async-start | bytes 6553600 | tf_op jit(solution)/shard_map/all_gather | solution.py:283
  3287.6 584.6 %all-gather.46.cloned.1.call-start = ((), (), s32[]{:S(2)}) async-start(), calls=%async_computation.34 | async-start | bytes 18350080 | tf_op jit(solution)/shard_map/all_gather | solution.py:291
  3288.1 864.1 %all-gather.42.cloned.1.call-start = ((), (), s32[]{:S(2)}) async-start(), calls=%async_computation.30 | async-start | bytes 18350080 | tf_op jit(solution)/shard_map/all_gather | solution.py:289
  3288.7 1115.6 %all-gather.44.cloned.1.call-start = ((), (), s32[]{:S(2)}) async-start(), calls=%async_computation.32 | async-start | bytes 18350080 | tf_op jit(solution)/shard_map/all_gather | solution.py:290
  3290.1 5.6 copy-start.16
  3291.2 110.5 %all-to-all-start.1 = ((bf16[256,4,640]{2,0,1:T(8,128)(2,1)}), bf16[256,4,640]{2,0,1:T(8,128)(2,1)}, u32[]{:S(2)}, u32[]{:S(2)}) async-start(bf16[256,4,640]{2,0,1:T(8,128)(2,1)} %bitcast.217), calls=%async_computation.6 | async-start | bytes 2621440 | tf_op jit(solution)/shard_map/all_to_all | solution.py:278
  3295.6 7.5 copy-start.20
  3295.6 1245.0 %reduce-scatter.31.cloned.1.call-start = ((), (), s32[]{:S(2)}) async-start(), calls=%async_computation.38 | async-start | bytes 1351680
  3295.6 7.4 copy-start.17
  3303.0 2.3 copy-start.19
  3310.0 1277.1 %reduce-scatter.25.cloned.1.call-start = ((), (), s32[]{:S(2)}) async-start(), calls=%async_computation.29 | async-start | bytes 3686400 | tf_op jit(solution)/shard_map/reduce_scatter | solution.py:312
  3409.9 1216.0 %reduce-scatter.23.cloned.1.call-start = ((), (), s32[]{:S(2)}) async-start(), calls=%async_computation.27 | async-start | bytes 921600 | tf_op jit(solution)/shard_map/reduce_scatter | solution.py:309
  3469.0 1195.4 %reduce-scatter.21.cloned.1.call-start = ((), (), s32[]{:S(2)}) async-start(), calls=%async_computation.26 | async-start | bytes 921600 | tf_op jit(solution)/shard_map/reduce_scatter | solution.py:306
  3497.2 1217.8 %reduce-scatter.19.cloned.1.call-start = ((), (), s32[]{:S(2)}) async-start(), calls=%async_computation.24 | async-start | bytes 3686400 | tf_op jit(solution)/shard_map/reduce_scatter | solution.py:303
  3599.8 1194.2 %reduce-scatter.33.cloned.1.call-start = ((), (), s32[]{:S(2)}) async-start(), calls=%async_computation.39 | async-start | bytes 10321920
  3902.5 970.2 %reduce-scatter.27.cloned.1.call-start = ((), (), s32[]{:S(2)}) async-start(), calls=%async_computation.31 | async-start | bytes 10321920 | tf_op jit(solution)/shard_map/reduce_scatter | solution.py:315
  4169.6 782.1 %reduce-scatter.29.cloned.1.call-start = ((), (), s32[]{:S(2)}) async-start(), calls=%async_computation.33 | async-start | bytes 10321920 | tf_op jit(solution)/shard_map/reduce_scatter | solution.py:318
  4423.0 31.3 copy-start.33
  (15 other events, 21.4 us)
Sparse Core Ops, SparseCore 0:
  9.6 68.3 all-gather.23
  79.5 64.2 all-gather.21
  146.0 31.4 all-gather.49
  179.5 31.6 all-gather.47
  212.6 225.7 all-gather.25
  439.9 224.9 all-gather.27
  666.5 612.5 all-gather.29
  1280.6 1213.6 all-gather.31
  2495.9 612.6 all-gather.33
  3158.7 50.8 reduce-scatter.16
  3222.9 50.5 reduce-scatter.14
  3275.0 126.6 all-gather.39
  3403.8 56.0 all-gather.51
  3461.9 31.8 all-gather.37
  3495.7 96.2 all-gather.35
  3593.4 278.6 all-gather.45
  3873.5 278.6 all-gather.41
  4153.6 250.6 all-gather.43
  4407.1 133.4 reduce-scatter.30
  4544.3 42.8 reduce-scatter.24
  4591.4 34.4 reduce-scatter.22
  4629.8 34.4 reduce-scatter.20
  4668.1 46.8 reduce-scatter.18
  4718.9 75.0 reduce-scatter.32
  4797.7 75.0 reduce-scatter.26
  4876.6 75.0 reduce-scatter.28
